TPU v7x, 256 devices: a whole 4x4x8 slice. The times are simulated.
256 devices in a mesh: region: 32 (over z, x), cell: 8 (over y, core).
Axes of the slice: x: 4, y: 4, z: 8, core: 2. Of those that a mesh axis runs over, the one named last changes fastest.
Arguments:
- points: float32 [3, 2097152], P(None, ('region', 'cell')), may hold values from -1951 to 1951
- cell_counts: int32 [8192], P(('region', 'cell')), may hold values from 192 to 256
- pair_cells: int32 [2, 106496], P(None, ('region', 'cell')), may hold values from 0 to 31, as said below
- pair_counts: int32 [256], P(('region', 'cell')), may hold values from 32 to 416, as said below
- nugget: float32 [2097152], P(('region', 'cell')), may hold values from 0.1 to 1
- solution: float32 [16, 2097152], P(None, ('region', 'cell')), may hold values from -6 to 6
- residual: float32 [16, 2097152], P(None, ('region', 'cell')), may hold values from -12 to 12
- direction: float32 [16, 2097152], P(None, ('region', 'cell')), may hold values from -12 to 12
- ritz_basis: float32 [32, 2097152], P(None, ('region', 'cell')), may hold values from -1.5 to 1.5
- ritz_image: float32 [32, 2097152], P(None, ('region', 'cell')), may hold values from -0.00390625 to 0.00390625
- inverse_gram: float32 [32, 32], replicated, may hold values from -1 to 1
Outputs:
- solution_out: float32 [16, 2097152], P(None, ('region', 'cell'))
- residual_out: float32 [16, 2097152], P(None, ('region', 'cell'))
- direction_out: float32 [16, 2097152], P(None, ('region', 'cell'))
Inputs may be any that keep to these rules, and one draw needn't show every extreme that they name: `pair_cells`: for each device, column s of its 416 columns is used if s < pair_counts of that device; used columns come first and unused ones hold (0, 0). Row 0 is a cell of that device (0 to 31), row 1 the distance in the cell order to the pair's second cell, 0 to 12; the second cell exists. Each cell is paired with itself exactly once and with the cells that directly follow it up to its last partner, at most 12 of them; used pairs are distinct. Points of two cells that are not paired are more than distance 1 apart. `pair_counts`: some device uses all 416 slots.
All inputs are finite; a program needn't handle non-finite values.
Results may differ from a plain program's by a relative error of at most 0.0025.
Values sent between devices are 32-bit elements; how exact they have to be, the bound alone decides.
No kernel may reach another device: no remote copies, remote signals or barrier semaphores. Data moves between devices by JAX's collectives and lax.ppermute only.
A program may use at most 64 MiB of HBM per device.

v0:
```python
import jax
import jax.numpy as jnp
from jax import lax
from jax.sharding import PartitionSpec as P

PTS = 256
REACH = 12


def passed_along(array, axis, by):
    length = lax.axis_size(axis)
    pairs = [(i, i + by) for i in range(length) if 0 <= i + by < length]
    return lax.ppermute(array, axis, pairs)


def wendland(distance):
    inner = jnp.maximum(1.0 - distance, 0.0)
    square = inner * inner
    return square * square * (4.0 * distance + 1.0)


def pair_terms(coords_ext, dirs_ext, first_cell, second_cell, in_use):
    coords_first = jnp.take(coords_ext, first_cell, axis=1)
    coords_second = jnp.take(coords_ext, second_cell, axis=1)
    gap_vec = coords_first[:, :, :, None] - coords_second[:, :, None, :]
    distance = jnp.sqrt(jnp.sum(gap_vec * gap_vec, axis=0))
    kernel_tile = (wendland(distance) * in_use[:, None, None]).astype(jnp.bfloat16)
    dir_first = jnp.take(dirs_ext, first_cell, axis=1)
    dir_second = jnp.take(dirs_ext, second_cell, axis=1)
    to_first = jnp.einsum(
        "bij,kbj->kbi", kernel_tile, dir_second, preferred_element_type=jnp.float32
    )
    to_second = jnp.einsum(
        "bij,kbi->kbj", kernel_tile, dir_first, preferred_element_type=jnp.float32
    )
    apart = (first_cell != second_cell).astype(jnp.float32)
    return (to_first, to_second * apart[None, :, None])


def pair_products(coords_ext, dirs_ext, first_cell, second_cell, used_count):
    per_turn = 16
    total_slots = first_cell.shape[0]
    padded = -(-total_slots // per_turn) * per_turn
    extra = jnp.zeros((padded - total_slots,), jnp.int32)
    first_all = jnp.concatenate([first_cell, extra])
    second_all = jnp.concatenate([second_cell, extra])
    totals_zero = jnp.zeros(dirs_ext.shape, jnp.float32)
    turn_count = (used_count + per_turn - 1) // per_turn

    def one_turn(turn, totals):
        begin_at = turn * per_turn
        first_now = lax.dynamic_slice_in_dim(first_all, begin_at, per_turn)
        second_now = lax.dynamic_slice_in_dim(second_all, begin_at, per_turn)
        in_use = (begin_at + jnp.arange(per_turn, dtype=jnp.int32) < used_count).astype(jnp.float32)
        to_first, to_second = pair_terms(coords_ext, dirs_ext, first_now, second_now, in_use)
        totals = totals.at[:, first_now].add(to_first)
        return totals.at[:, second_now].add(to_second)

    return lax.fori_loop(0, turn_count, one_turn, totals_zero)


def local_dot(left, right):
    return jnp.sum(left * right, axis=(1, 2))


def project(images, field):
    flat = field.reshape(field.shape[0], -1)
    return lax.dot_general(images, flat, (((1,), (1,)), ((), ())), precision=lax.Precision.HIGHEST)


def local(
    points,
    cell_counts,
    pair_cells,
    pair_counts,
    nugget,
    solution,
    residual,
    direction,
    ritz_basis,
    ritz_image,
    inverse_gram,
):
    cells_dev = cell_counts.shape[0]
    rhs_count = solution.shape[0]
    in_cell = (jnp.arange(PTS, dtype=jnp.int32)[None, :] < cell_counts[:, None]).astype(jnp.float32)
    dir_live = direction.reshape(rhs_count, cells_dev, PTS) * in_cell
    res_live = residual.reshape(rhs_count, cells_dev, PTS) * in_cell
    sol_live = solution.reshape(rhs_count, cells_dev, PTS) * in_cell
    coords = points.reshape(3, cells_dev, PTS)
    stacked = jnp.concatenate([coords, dir_live], axis=0)
    pieces = [stacked]
    hop = 1
    piece_width = min(cells_dev, REACH - (hop - 1) * cells_dev)
    piece_widths = [piece_width]
    pieces.append(passed_along(stacked[:, :piece_width], ("region", "cell"), -hop))
    extended = jnp.concatenate(pieces, axis=1)
    first_cell = pair_cells[0]
    second_cell = first_cell + pair_cells[1]
    totals = pair_products(
        extended[:3], extended[3:].astype(jnp.bfloat16), first_cell, second_cell, pair_counts[0]
    )
    kernel_part = totals[:, :cells_dev]
    hop = 1
    piece_width = piece_widths[hop - 1]
    returned = passed_along(totals[:, cells_dev : cells_dev + piece_width], ("region", "cell"), hop)
    kernel_part = kernel_part.at[:, :piece_width].add(returned)
    image = in_cell * (nugget.reshape(cells_dev, PTS)[None] * dir_live + kernel_part)
    curvature, res_norm = lax.psum(
        (local_dot(dir_live, image), local_dot(res_live, res_live)), ("region", "cell")
    )
    step_len = res_norm / curvature
    residual_out = res_live - step_len[:, None, None] * image
    new_norm, projected = lax.psum(
        (local_dot(residual_out, residual_out), project(ritz_image, residual_out)),
        ("region", "cell"),
    )
    solution_out = sol_live + step_len[:, None, None] * dir_live
    coefficients = jnp.dot(inverse_gram, projected, precision=lax.Precision.HIGHEST)
    correction = lax.dot_general(
        coefficients, ritz_basis, (((0,), (0,)), ((), ())), precision=lax.Precision.HIGHEST
    )
    growth = new_norm / res_norm
    direction_out = in_cell * (
        growth[:, None, None] * dir_live
        + residual_out
        - correction.reshape(rhs_count, cells_dev, PTS)
    )
    return (
        solution_out.reshape(rhs_count, -1),
        residual_out.reshape(rhs_count, -1),
        direction_out.reshape(rhs_count, -1),
    )


def solution(mesh):
    in_specs = (
        P(None, ("region", "cell")),
        P(("region", "cell")),
        P(None, ("region", "cell")),
        P(("region", "cell")),
        P(("region", "cell")),
        P(None, ("region", "cell")),
        P(None, ("region", "cell")),
        P(None, ("region", "cell")),
        P(None, ("region", "cell")),
        P(None, ("region", "cell")),
        P(),
    )
    out_specs = (
        P(None, ("region", "cell")),
        P(None, ("region", "cell")),
        P(None, ("region", "cell")),
    )
    return jax.shard_map(local, mesh=mesh, in_specs=in_specs, out_specs=out_specs, check_vma=False)
```

profile of v0, /device:TPU:32, one launch (start us, length us, event | category | flops | bytes accessed | tf_op | source)
XLA Modules:
  0.0 711.9 jit_solution(7404535774035481001)
XLA Ops:
  3.8 6.1 collective-permute-start
  16.9 160.7 %while.11 = (s32[]{:T(128)}, f32[16,44,256]{2,0,1:T(8,128)}, s32[]{:T(128)}, s32[416]{0:T(512)}, s32[416]{0:T(512)}, /*index=5*/bf16[16,44,256]{2,0,1:T(8,128)(2...) while((s32[]{:T(128)}, f32[16,44,256]{2,0,1:T(8,128)}, ...), condition=%wide.region_6.9_spmd, body=%wide.region_2.8_spmd.sunk | while | flops 85289232 | bytes 18261356 | solution.py:59
  18.2 1.5 gather_fusion.1
  19.9 1.5 gather_fusion
  21.5 2.2 multiply_reduce_fusion.5
  24.4 2.2 multiply_convert_fusion.2
  26.6 1.5 gather_fusion.2
  29.4 2.5 scatter_fusion
  31.9 1.5 gather_fusion.3
  34.5 2.5 scatter_fusion.1
  38.3 1.5 gather_fusion.1
  41.5 2.2 multiply_reduce_fusion.5
  44.4 2.2 multiply_convert_fusion.2
  46.6 1.5 gather_fusion.2
  49.5 2.5 scatter_fusion
  52.0 1.5 gather_fusion.3
  54.6 2.5 scatter_fusion.1
  58.4 1.5 gather_fusion.1
  61.6 2.2 multiply_reduce_fusion.5
  64.5 2.2 multiply_convert_fusion.2
  66.7 1.5 gather_fusion.2
  69.6 2.6 scatter_fusion
  72.1 1.5 gather_fusion.3
  74.7 2.5 scatter_fusion.1
  78.5 1.5 gather_fusion.1
  81.8 2.2 multiply_reduce_fusion.5
  84.7 2.2 multiply_convert_fusion.2
  86.9 1.5 gather_fusion.2
  89.8 2.5 scatter_fusion
  92.3 1.5 gather_fusion.3
  94.8 2.5 scatter_fusion.1
  98.6 1.5 gather_fusion.1
  101.9 2.2 multiply_reduce_fusion.5
  104.8 2.2 multiply_convert_fusion.2
  107.0 1.5 gather_fusion.2
  109.8 2.5 scatter_fusion
  112.3 1.5 gather_fusion.3
  114.9 2.5 scatter_fusion.1
  118.7 1.5 gather_fusion.1
  122.0 2.2 multiply_reduce_fusion.5
  124.9 2.2 multiply_convert_fusion.2
  127.0 1.5 gather_fusion.2
  129.9 2.5 scatter_fusion
  132.4 1.5 gather_fusion.3
  135.0 2.5 scatter_fusion.1
  138.8 1.5 gather_fusion.1
  142.0 2.2 multiply_reduce_fusion.5
  144.9 2.2 multiply_convert_fusion.2
  147.1 1.5 gather_fusion.2
  150.0 2.5 scatter_fusion
  152.5 1.5 gather_fusion.3
  155.1 2.5 scatter_fusion.1
  158.9 1.5 gather_fusion.1
  162.1 2.2 multiply_reduce_fusion.5
  165.0 2.2 multiply_convert_fusion.2
  167.2 1.5 gather_fusion.2
  170.1 2.5 scatter_fusion
  172.6 1.5 gather_fusion.3
  175.2 2.5 scatter_fusion.1
  177.6 1.6 copy.32
  179.2 40.5 %collective-permute-start.1 = (f32[16,12,256]{2,1,0:T(8,128)S(1)}, f32[16,12,256]{2,1,0:T(8,128)S(1)}, u32[]{:S(2)}, u32[]{:S(2)}) collective-permute-start(f32[16,12,256]{2,1,0:T(8,128)S(1)} %slice.66), channel_id=1, source_target_pairs={{0,1},{1,2},{2,3},{3,4},{4,5},{5,6},{6,7},{7,8},{8,9},{9,10},{10,1... | collective-permute-start | bytes 589832 | tf_op jit(solution)/shard_map/ppermute | solution.py:13
  225.2 408.1 %all-reduce.1 = (f32[16]{0:T(128)S(1)}, f32[16]{0:T(128)S(1)}) all-reduce(f32[16]{0:T(128)S(1)} %multiply_reduce_fusion.3, f32[16]{0:T(128)S(1)} %multiply_reduce_fusion.2), channel_id=1, replica_groups=mesh['region'=32,'cell'=8] {'region','cell'}, use_global_device_ids=true, to_apply=%region_1.2 | all-reduce | flops 32 | bytes 256 | tf_op jit(solution)/shard_map/psum | solution.py:109
  633.9 2.3 convolution_bitcast_fusion
  636.3 72.5 %all-reduce = (f32[32,16]{0,1:T(8,128)S(1)}, f32[16]{0:T(128)S(1)}) all-reduce(f32[32,16]{0,1:T(8,128)S(1)} %convolution_bitcast_fusion, f32[16]{0:T(128)S(1)} %get-tuple-element.109), channel_id=1, replica_groups=mesh['region'=32,'cell'=8] {'region','cell'}, use_global_device_ids=true, to_apply=%region_11.14 | all-reduce | flops 528 | bytes 4224 | tf_op jit(solution)/shard_map/psum | solution.py:114
  (158 shorter events, 65.0 us)
Async XLA Ops:
  0.6 708.3 %copy-start = (f32[32,8192]{1,0:T(8,128)S(1)}, f32[32,8192]{1,0:T(8,128)}, u32[]{:S(2)}) copy-start(f32[32,8192]{1,0:T(8,128)} %param.27) | copy-start | bytes 3145732
  1.9 1.7 copy-start.1
  2.7 1.0 copy-start.5
  3.8 10.5 %collective-permute-start = (f32[19,12,256]{2,1,0:T(8,128)S(1)}, f32[19,12,256]{2,1,0:T(8,128)S(1)}, u32[]{:S(2)}, u32[]{:S(2)}) collective-permute-start(f32[19,12,256]{2,1,0:T(8,128)S(1)} %pad_maximum_fusion.1), channel_id=1, source_target_pairs={{1,0},{2,1},{3,2},{4,3},{5,4},{6,5},{7,6},{8,7},{9,8},{10,9},{11,1... | collective-permute-start | bytes 700424 | tf_op jit(solution)/shard_map/ppermute | solution.py:13
  18.2 8.4 %copy-start.8 = (pred[16]{0:T(512)(128)(4,1)}, pred[16]{0:T(512)(128)(4,1)S(1)}, u32[]{:S(2)}) copy-start(pred[16]{0:T(512)(128)(4,1)S(1)} %get-tuple-element.173) | copy-start | bytes 52 | tf_op jit(solution)/shard_map/while
  38.3 8.4 %copy-start.8 = (pred[16]{0:T(512)(128)(4,1)}, pred[16]{0:T(512)(128)(4,1)S(1)}, u32[]{:S(2)}) copy-start(pred[16]{0:T(512)(128)(4,1)S(1)} %get-tuple-element.173) | copy-start | bytes 52 | tf_op jit(solution)/shard_map/while
  58.3 8.4 %copy-start.8 = (pred[16]{0:T(512)(128)(4,1)}, pred[16]{0:T(512)(128)(4,1)S(1)}, u32[]{:S(2)}) copy-start(pred[16]{0:T(512)(128)(4,1)S(1)} %get-tuple-element.173) | copy-start | bytes 52 | tf_op jit(solution)/shard_map/while
  78.5 8.4 %copy-start.8 = (pred[16]{0:T(512)(128)(4,1)}, pred[16]{0:T(512)(128)(4,1)S(1)}, u32[]{:S(2)}) copy-start(pred[16]{0:T(512)(128)(4,1)S(1)} %get-tuple-element.173) | copy-start | bytes 52 | tf_op jit(solution)/shard_map/while
  98.6 8.4 %copy-start.8 = (pred[16]{0:T(512)(128)(4,1)}, pred[16]{0:T(512)(128)(4,1)S(1)}, u32[]{:S(2)}) copy-start(pred[16]{0:T(512)(128)(4,1)S(1)} %get-tuple-element.173) | copy-start | bytes 52 | tf_op jit(solution)/shard_map/while
  118.7 8.4 %copy-start.8 = (pred[16]{0:T(512)(128)(4,1)}, pred[16]{0:T(512)(128)(4,1)S(1)}, u32[]{:S(2)}) copy-start(pred[16]{0:T(512)(128)(4,1)S(1)} %get-tuple-element.173) | copy-start | bytes 52 | tf_op jit(solution)/shard_map/while
  138.8 8.4 %copy-start.8 = (pred[16]{0:T(512)(128)(4,1)}, pred[16]{0:T(512)(128)(4,1)S(1)}, u32[]{:S(2)}) copy-start(pred[16]{0:T(512)(128)(4,1)S(1)} %get-tuple-element.173) | copy-start | bytes 52 | tf_op jit(solution)/shard_map/while
  158.9 8.4 %copy-start.8 = (pred[16]{0:T(512)(128)(4,1)}, pred[16]{0:T(512)(128)(4,1)S(1)}, u32[]{:S(2)}) copy-start(pred[16]{0:T(512)(128)(4,1)S(1)} %get-tuple-element.173) | copy-start | bytes 52 | tf_op jit(solution)/shard_map/while
  177.6 46.1 %copy-start.2 = (f32[2,8,32,256]{3,2,1,0:T(8,128)S(1)}, f32[2,8,32,256]{3,2,1,0:T(8,128)}, u32[]{:S(2)}) copy-start(f32[2,8,32,256]{3,2,1,0:T(8,128)} %copy-done.1) | copy-start | bytes 1572868
  177.6 46.1 %copy-start.6 = (f32[32,256]{1,0:T(8,128)S(1)}, f32[32,256]{1,0:T(8,128)}, u32[]{:S(2)}) copy-start(f32[32,256]{1,0:T(8,128)} %copy-done.5) | copy-start | bytes 98308
  179.2 44.1 %collective-permute-start.1 = (f32[16,12,256]{2,1,0:T(8,128)S(1)}, f32[16,12,256]{2,1,0:T(8,128)S(1)}, u32[]{:S(2)}, u32[]{:S(2)}) collective-permute-start(f32[16,12,256]{2,1,0:T(8,128)S(1)} %slice.66), channel_id=1, source_target_pairs={{0,1},{1,2},{2,3},{3,4},{4,5},{5,6},{6,7},{7,8},{8,9},{9,10},{10,1... | collective-permute-start | bytes 589832 | tf_op jit(solution)/shard_map/ppermute | solution.py:13
  223.3 485.5 %copy-start.9 = (f32[32,32]{1,0:T(8,128)S(1)}, f32[32,32]{1,0:T(8,128)}, u32[]{:S(2)}) copy-start(f32[32,32]{1,0:T(8,128)} %param.29) | copy-start | bytes 12292
  633.6 77.3 %copy-start.4 = (f32[16,8192]{1,0:T(8,128)S(1)}, f32[16,8192]{1,0:T(8,128)}, u32[]{:S(2)}) copy-start(f32[16,8192]{1,0:T(8,128)} %param.26) | copy-start | bytes 1572868
  633.9 77.9 %copy-start.3 = (f32[2,8,32,256]{3,1,2,0:T(8,128)}, f32[2,8,32,256]{3,1,2,0:T(8,128)S(1)}, u32[]{:S(2)}) copy-start(f32[2,8,32,256]{3,1,2,0:T(8,128)S(1)} %copy.39) | copy-start | bytes 1572868
  708.7 2.2 copy-start.7
where the time goes:
time: 723 us; the launch traced here: 712 us
  blocking collectives  481 us (67%)
  other arithmetic  97.9 us (14%)
  local copies, waits for them, and re-layouts  62.3 us (9%)
  starting transfers between devices  46.6 us (6%)
  matrix products  21.7 us (3%)
    psum x1, blocking collectives, local(): lax.psum((local_dot(dir_live, image), local_dot(res_live, res_live)), ('r...  408 us
    psum x1, blocking collectives, local(): lax.psum((local_dot(residual_out, residual_out), project(ritz_image, resi...  72.5 us
    ppermute x2, starting transfers between devices, passed_along(): return lax.ppermute(array, axis, pairs)  46.6 us
    scatter-add x8, other arithmetic, one_turn(): totals = totals.at[:, first_now].add(to_first)  20.1 us
    scatter-add x8, other arithmetic, one_turn(): return totals.at[:, second_now].add(to_second)  19.8 us
    reduce_sum x8, other arithmetic, pair_terms(): distance = jnp.sqrt(jnp.sum(gap_vec * gap_vec, axis=0))  17.9 us
    convert_element_type x8, other arithmetic, pair_terms(): (wendland(distance) * in_use[:, None, None]).astype(jnp.bfloat16)  17.4 us
  transfers between devices with their start and end apart: 2, of which 1 were waited for; matrix products, arithmetic and copies ran while one was open for 1% of the time, Pallas kernels for 0%

commit v1 on v0

v1 whole, which is shorter than its diff:
```python
import jax
import jax.numpy as jnp
from jax import lax
from jax.experimental import pallas as pl
from jax.experimental.pallas import tpu as pltpu
from jax.sharding import PartitionSpec as P

PTS = 256
REACH = 12
KF = 48
FAR = 1e18
ROOM = 16.0
AXES = ("region", "cell")
F32 = jnp.float32
BF16 = jnp.bfloat16


def mm(x, y):
    return lax.dot_general(x, y, (((1,), (0,)), ((), ())), preferred_element_type=F32)


def mm_t(x, y):
    return lax.dot_general(x, y, (((1,), (1,)), ((), ())), preferred_element_type=F32)


def high(x):
    return x.astype(BF16).astype(F32)


def split3(x):
    h = high(x)
    m = high(x - h)
    return h, m, high(x - h - m)


def tile_of(scaled_square):
    s = jnp.maximum(scaled_square, 1e-30)
    t = s * lax.rsqrt(s)
    u = jnp.maximum(4.0 - t, 0.0)
    u2 = u * u
    return ((u2 * u2) * (t + 1.0)).astype(BF16)


def cols(block, size=PTS):
    return pl.ds(pl.multiple_of(block * size, size), size)


def with_norm(vec):
    row = lax.broadcasted_iota(jnp.int32, vec.shape, 0)
    return row, jnp.sum(vec * vec, axis=0, keepdims=True)


def weights_side(p):
    row, norm = with_norm(p)
    a = jnp.where(row == 3, norm, -2.0 * p)
    h, m, l = split3(a)
    one_h = jnp.where(row == 3, 1.0, h)
    one_m = jnp.where(row == 3, 1.0, m)
    return jnp.concatenate([h, m, one_h, one_m, l, one_h], axis=0).astype(BF16)


def rows_side(q):
    row, norm = with_norm(q)
    a = jnp.where(row == 3, norm, q)
    h, m, l = split3(a)
    one = jnp.where(row == 3, 1.0, h)
    mid_h = jnp.where(row == 3, h, m)
    return jnp.concatenate([one, one, mid_h, m, one, l], axis=0), norm


def pair_kernel(
    cells,
    halo_cells,
    cnt,
    hcnt,
    pts,
    dirs,
    hdirs,
    hpts,
    own,
    halo,
    off,
    dc,
    pc,
    db,
    fs,
    cen,
    acc_i,
    acc_j,
    f0,
    f1,
    s0,
    s1,
    w0,
    w1,
    tab_v,
    tab_s,
    sem,
):
    blocks = cells + halo_cells
    spare = blocks
    lane1 = lax.broadcasted_iota(jnp.int32, (1, PTS), 1)
    lane128 = lax.broadcasted_iota(jnp.int32, (1, 128), 1)
    dc[...] = jnp.zeros_like(dc)
    pc[...] = jnp.zeros_like(pc)
    acc_i[...] = jnp.zeros_like(acc_i)
    acc_j[...] = jnp.zeros_like(acc_j)

    def place(c, at, count, dref, pref):
        shift = at % 128
        base = pl.multiple_of((at // 128) * 128, 128)
        live = lane1 < count
        dv = jnp.where(live, dref[:, cols(c)], 0.0)
        pv = jnp.where(live, pref[:, cols(c)], 0.0)
        for ref, val in ((dc, dv), (pc, pv)):
            rows = val.shape[0]
            wide = jnp.concatenate([val, jnp.zeros((rows, 128), F32)], axis=1)
            wide = pltpu.roll(wide, shift, 1)
            old = ref[:rows, pl.ds(base, 128)]
            ref[:rows, pl.ds(base, 128)] = jnp.where(lane128 < shift, old, wide[:, :128])
            ref[:rows, pl.ds(base + 128, 256)] = wide[:, 128:]
        return at + count

    def place_own(c, at):
        off[c] = at
        return place(c, at, cnt[c], dirs, pts)

    own_end = lax.fori_loop(0, cells, place_own, jnp.int32(0))
    strips = (own_end + (PTS - 1)) // PTS
    halo_at = strips * PTS

    def place_halo(c, at):
        off[cells + c] = at
        return place(c, at, hcnt[c], hdirs, hpts)

    halo_end = lax.fori_loop(0, halo_cells, place_halo, halo_at)
    db[...] = dc[...].astype(BF16)

    def prepare(j, carry):
        low, top, far = carry
        here = pc[:, cols(j)]
        at = j * PTS + lane1
        valid = (at < own_end) | ((at >= halo_at) & (at < halo_end))
        lo = jnp.min(jnp.where(valid, here, FAR), axis=1, keepdims=True)
        hi = jnp.max(jnp.where(valid, here, -FAR), axis=1, keepdims=True)
        centre = jnp.where(lo <= hi, 0.5 * (lo + hi), 0.0)
        cen[pl.ds(pl.multiple_of(j * 8, 8), 8), :] = jnp.broadcast_to(centre, (8, 128))
        feats, norm = rows_side(4.0 * (here - centre))
        fs[cols(j), :] = feats.T.astype(BF16)
        low = jnp.where(lane128 == j, lo, low)
        top = jnp.where(lane128 == j, hi, top)
        return low, top, jnp.maximum(far, jnp.where(valid, norm, 0.0))

    start = (
        jnp.full((8, 128), FAR, F32),
        jnp.full((8, 128), -FAR, F32),
        jnp.zeros((1, PTS), F32),
    )
    low, top, far = lax.fori_loop(0, blocks, prepare, start)
    cen[pl.ds(blocks * 8, 8), :] = jnp.zeros((8, 128), F32)
    fs[pl.ds(blocks * PTS, PTS), :] = jnp.zeros((PTS, KF), BF16)
    square = lambda v: jnp.concatenate([v, jnp.zeros((120, 128), F32)], axis=0).T
    low_t, top_t = square(low), square(top)
    gap2 = jnp.zeros((128, 128), F32)
    for k in range(3):
        gap = jnp.maximum(low[k : k + 1] - top_t[:, k : k + 1], low_t[:, k : k + 1] - top[k : k + 1])
        gap = jnp.maximum(gap, 0.0)
        gap2 = gap2 + gap * gap
    ri = lax.broadcasted_iota(jnp.int32, (128, 128), 0)
    rj = lax.broadcasted_iota(jnp.int32, (128, 128), 1)
    need = (gap2 <= 1.001) & (rj > ri)
    stop = jnp.max(jnp.where(need, rj + 1, ri + 1).astype(F32), axis=1, keepdims=True)
    stop = jnp.broadcast_to(stop, (128, 128)).T[:8].astype(jnp.int32)
    radius = jnp.max(far, axis=1, keepdims=True)
    spread = jnp.where(radius > 16.0 * ROOM, 1, 0)
    tab_v[...] = jnp.where(lane128 == 127, spread, stop)
    copy = pltpu.make_async_copy(tab_v, tab_s, sem)
    copy.start()
    copy.wait()

    def following(i, j):
        n = j + 1
        over = n >= tab_s[0, i]
        up = jnp.where(i + 1 >= strips, spare, i + 1)
        return jnp.where(over, up, i), jnp.where(over, up, n)

    def stage0(i, j, f):
        c = cen[pl.ds(pl.multiple_of(j * 8, 8), 8), :]
        f[...] = weights_side(4.0 * (pc[:, cols(i)] - jnp.concatenate([c, c], axis=1)))

    def stage1(j, f, s):
        s[...] = mm(fs[cols(j), :], f[...])

    def stage2(s, w):
        w[...] = tile_of(s[...])

    def stage3(i, j, w):
        tile = w[...]
        acc_i[:, cols(i)] += mm(db[:, cols(j)], tile)
        keep = jnp.where(j > i, 1.0, 0.0)
        acc_j[:, cols(j)] += mm_t(db[:, cols(i)], tile) * keep

    zero = jnp.int32(0)
    last = jnp.int32(spare)
    total = lax.fori_loop(0, strips, lambda i, n: n + tab_s[0, i] - i, zero)

    @pl.when(tab_s[0, 127] == 0)
    def _():
        w1[...] = jnp.zeros_like(w1)
        ib, jb = following(zero, zero)
        stage0(zero, zero, f0)
        stage1(zero, f0, s0)
        stage0(ib, jb, f1)

        def two(_, carry):
            ia, ja, i0, j0, i1, j1 = carry
            i2, j2 = following(i1, j1)
            stage0(i2, j2, f0)
            stage1(j1, f1, s1)
            stage2(s0, w0)
            stage3(ia, ja, w1)
            i3, j3 = following(i2, j2)
            stage0(i3, j3, f1)
            stage1(j2, f0, s0)
            stage2(s1, w1)
            stage3(i0, j0, w0)
            return i1, j1, i2, j2, i3, j3

        lax.fori_loop(0, total // 2 + 1, two, (last, last, zero, zero, ib, jb))

    @pl.when(tab_s[0, 127] != 0)
    def _():
        def one(_, carry):
            i, j = carry
            pj = pc[:, cols(j)].T
            pi = pc[:, cols(i)]
            for h in range(0, PTS, 64):
                s = jnp.zeros((64, PTS), F32)
                for k in range(3):
                    d = 4.0 * (pj[h : h + 64, k : k + 1] - pi[k : k + 1, :])
                    s = s + d * d
                w0[pl.ds(h, 64), :] = tile_of(s)
            stage3(i, j, w0)
            return following(i, j)

        lax.fori_loop(0, total, one, (zero, zero))

    def take(c, count, ref, k):
        at = off[k]
        base = pl.multiple_of((at // 128) * 128, 128)
        both = acc_i[:, pl.ds(base, 384)] + acc_j[:, pl.ds(base, 384)]
        back = pltpu.roll(both, 384 - at % 128, 1)[:, :PTS] * (1.0 / 256.0)
        ref[:, cols(c)] = jnp.where(lane1 < count, back, 0.0)

    def take_own(c, _):
        take(c, cnt[c], own, c)
        return 0

    def take_halo(c, _):
        take(c, hcnt[c], halo, cells + c)
        return 0

    lax.fori_loop(0, cells, take_own, 0)
    lax.fori_loop(0, halo_cells, take_halo, 0)


VM = pl.BlockSpec(memory_space=pltpu.VMEM)
SM = pl.BlockSpec(memory_space=pltpu.SMEM)
BIG = pltpu.CompilerParams(vmem_limit_bytes=56 << 20)


def pair_products(counts, halo_counts, points, direction, halo_dirs, halo_points):
    cells, halo_cells = counts.shape[0], halo_counts.shape[0]
    rhs = direction.shape[0]
    blocks = cells + halo_cells + 1
    wide = blocks * PTS + 256

    def kernel(*refs):
        pair_kernel(cells, halo_cells, *refs)

    return pl.pallas_call(
        kernel,
        name="pairs",
        out_shape=[
            jax.ShapeDtypeStruct((rhs, cells * PTS), F32),
            jax.ShapeDtypeStruct((rhs, halo_cells * PTS), F32),
        ],
        in_specs=[SM, SM, VM, VM, VM, VM],
        out_specs=[VM, VM],
        scratch_shapes=[
            pltpu.SMEM((cells + halo_cells,), jnp.int32),
            pltpu.VMEM((rhs, wide), F32),
            pltpu.VMEM((8, wide), F32),
            pltpu.VMEM((rhs, wide), BF16),
            pltpu.VMEM((blocks * PTS, KF), BF16),
            pltpu.VMEM((blocks * 8, 128), F32),
            pltpu.VMEM((rhs, wide), F32),
            pltpu.VMEM((rhs, wide), F32),
            pltpu.VMEM((KF, PTS), BF16),
            pltpu.VMEM((KF, PTS), BF16),
            pltpu.VMEM((PTS, PTS), F32),
            pltpu.VMEM((PTS, PTS), F32),
            pltpu.VMEM((PTS, PTS), BF16),
            pltpu.VMEM((PTS, PTS), BF16),
            pltpu.VMEM((8, 128), jnp.int32),
            pltpu.SMEM((8, 128), jnp.int32),
            pltpu.SemaphoreType.DMA,
        ],
        compiler_params=BIG,
    )(counts, halo_counts, points, direction, halo_dirs, halo_points)


def sums_kernel(cnt, own, back, nug, dirs, res, ritz, image, sums):
    cells = own.shape[1] // PTS
    halo_cells = back.shape[1] // PTS
    lane1 = lax.broadcasted_iota(jnp.int32, (1, PTS), 1)

    def of_cell(c, part, extra):
        live = lane1 < cnt[c]
        d = jnp.where(live, dirs[:, cols(c)], 0.0)
        r = jnp.where(live, res[:, cols(c)], 0.0)
        k = own[:, cols(c)]
        if extra:
            k = k + back[:, cols(c)]
        im = jnp.where(live, nug[:, cols(c)] * d + k, 0.0)
        image[:, cols(c)] = im
        dk, rr, ri, ii, prod = part
        both = jnp.concatenate([r, im], axis=0)
        bh = high(both)
        z = ritz[:, cols(c)]
        zh = high(z)
        left = jnp.concatenate([bh, both - bh], axis=0).astype(BF16)
        right = jnp.concatenate([zh, z - zh], axis=0).astype(BF16)
        return dk + d * im, rr + r * r, ri + r * im, ii + im * im, prod + mm_t(left, right)

    rhs = own.shape[0]
    zero = jnp.zeros((rhs, PTS), F32)
    part = (zero, zero, zero, zero, jnp.zeros((4 * rhs, 2 * ritz.shape[0]), F32))
    part = lax.fori_loop(0, halo_cells, lambda c, p: of_cell(c, p, True), part)
    part = lax.fori_loop(halo_cells, cells, lambda c, p: of_cell(c, p, False), part)
    dots = [jnp.sum(p, axis=1, keepdims=True) for p in part[:4]]
    prod = part[4]
    n = ritz.shape[0]
    h = 2 * rhs
    prod = prod[:h, :n] + prod[:h, n:] + prod[h:, :n]
    sums[...] = jnp.zeros_like(sums)
    sums[:, :n] = prod[:rhs]
    sums[:, n : 2 * n] = prod[rhs:]
    for k in range(4):
        sums[:, 2 * n + k : 2 * n + k + 1] = dots[k]


def local_sums(counts, own, back, nugget, direction, residual, ritz_image):
    return pl.pallas_call(
        sums_kernel,
        name="sums",
        out_shape=[
            jax.ShapeDtypeStruct(own.shape, F32),
            jax.ShapeDtypeStruct((own.shape[0], 128), F32),
        ],
        in_specs=[SM] + [VM] * 6,
        out_specs=[VM, VM],
        compiler_params=BIG,
    )(counts, own, back, nugget, direction, residual, ritz_image)


def finish_kernel(cnt, sums, gram, image, dirs, res, sol, basis, sol_out, res_out, dir_out):
    cells = image.shape[1] // PTS
    n = gram.shape[0]
    lane1 = lax.broadcasted_iota(jnp.int32, (1, PTS), 1)
    curvature, rr, ri, ii = (sums[:, 2 * n + k : 2 * n + k + 1] for k in range(4))
    step = rr / curvature
    growth = (rr + step * (step * ii - 2.0 * ri)) / rr
    projected = sums[:, :n] - step * sums[:, n : 2 * n]
    coef = lax.dot_general(
        projected,
        gram[...],
        (((1,), (1,)), ((), ())),
        precision=lax.Precision.HIGHEST,
        preferred_element_type=F32,
    )
    ch = high(coef)
    left = jnp.concatenate([ch, ch, coef - ch], axis=1).astype(BF16)

    def of_cell(c, _):
        live = lane1 < cnt[c]
        d = jnp.where(live, dirs[:, cols(c)], 0.0)
        r = jnp.where(live, res[:, cols(c)], 0.0)
        s = jnp.where(live, sol[:, cols(c)], 0.0)
        b = basis[:, cols(c)]
        bh = high(b)
        right = jnp.concatenate([bh, b - bh, bh], axis=0).astype(BF16)
        new = r - step * image[:, cols(c)]
        sol_out[:, cols(c)] = s + step * d
        res_out[:, cols(c)] = new
        dir_out[:, cols(c)] = jnp.where(live, growth * d + new - mm(left, right), 0.0)
        return 0

    lax.fori_loop(0, cells, of_cell, 0)


def finish(counts, sums, gram, image, direction, residual, solution, basis):
    return pl.pallas_call(
        finish_kernel,
        name="finish",
        out_shape=[jax.ShapeDtypeStruct(image.shape, F32)] * 3,
        in_specs=[SM] + [VM] * 7,
        out_specs=[VM] * 3,
        compiler_params=BIG,
    )(counts, sums, gram, image, direction, residual, solution, basis)


def passed_along(array, by):
    length = lax.axis_size(AXES)
    pairs = [(i, i + by) for i in range(length) if 0 <= i + by < length]
    return lax.ppermute(array, AXES, pairs)


def summed(array):
    for axis in ("cell", "region"):
        copies = jnp.broadcast_to(array[None], (lax.axis_size(axis),) + array.shape)
        array = jnp.sum(lax.all_to_all(copies, axis, 0, 0), axis=0)
    return array


def local(
    points,
    cell_counts,
    pair_cells,
    pair_counts,
    nugget,
    solution,
    residual,
    direction,
    ritz_basis,
    ritz_image,
    inverse_gram,
):
    width = min(cell_counts.shape[0], REACH)
    halo_counts = passed_along(cell_counts[:width], -1)
    halo_dirs = passed_along(direction[:, : width * PTS], -1)
    halo_points = passed_along(points[:, : width * PTS], -1)
    own, beyond = pair_products(
        cell_counts, halo_counts, points, direction, halo_dirs, halo_points
    )
    back = passed_along(beyond, 1)
    image, sums = local_sums(
        cell_counts, own, back, nugget.reshape(1, -1), direction, residual, ritz_image
    )
    return tuple(
        finish(
            cell_counts,
            summed(sums),
            inverse_gram,
            image,
            direction,
            residual,
            solution,
            ritz_basis,
        )
    )


def solution(mesh):
    split = P(None, AXES)
    line = P(AXES)
    in_specs = (split, line, split, line, line, split, split, split, split, split, P())
    return jax.shard_map(
        local, mesh=mesh, in_specs=in_specs, out_specs=(split,) * 3, check_vma=False
    )
```

time: 723 us -> 134 us (0.19); the launches traced: 712 us -> 133 us
  blocking collectives: 481 us -> 59.2 us
  other arithmetic: 97.9 us -> 0.63 us
  local copies, waits for them, and re-layouts: 62.3 us -> 4.44 us
  Pallas kernels: 0 us -> 44.6 us
  starting transfers between devices: 46.6 us -> 14.5 us
  matrix products: 21.7 us -> 0 us
  waiting for transfers between devices: 0.48 us -> 8.92 us
    psum x2 -> x0, blocking collectives: 481 us -> none  [the longest x1 408 us: local(): lax.psum((local_dot(dir_live, image), local_dot(res_live, res_live)), ('r...]
    all_to_all x0 -> x2, blocking collectives: none -> 59.2 us  [summed(): array = jnp.sum(lax.all_to_all(copies, axis, 0, 0), axis=0)]
    gather x32 -> x0, local copies, waits for them, and re-layouts: 48.9 us -> none  [the longest x8 12.3 us: pair_terms(): dir_second = jnp.take(dirs_ext, second_cell, axis=1)]
    pallas_call x0 -> x3, Pallas kernels: none -> 44.6 us  [the longest x1 29.9 us: pair_products(): pl.pallas_call(kernel, name='pairs', out_shape=[jax.ShapeDtypeStruct((rhs...]
    scatter-add x16 -> x0, other arithmetic: 39.9 us -> none  [the longest x8 20.1 us: one_turn(): totals = totals.at[:, first_now].add(to_first)]
    ppermute x2 -> x4, starting transfers between devices: 46.6 us -> 14.5 us  [passed_along(): return lax.ppermute(array, AXES, pairs)]
    convert_element_type x18 -> x0, other arithmetic: 24.1 us -> none  [the longest x8 17.4 us: pair_terms(): (wendland(distance) * in_use[:, None, None]).astype(jnp.bfloat16)]
    dot_general x19 -> x0, matrix products: 21.7 us -> none  [the longest x8 10.5 us: pair_terms(): jnp.einsum('bij,kbj->kbi', kernel_tile, dir_second, preferred_element_typ...]
  transfers between devices with their start and end apart: 2 -> 4, of which waited for: 1 -> 2; matrix products, arithmetic and copies ran while one was open for 1% -> 1% of each run, Pallas kernels for 0% -> 0%
where the time goes in v1:
time: 134 us; the launch traced here: 133 us
  blocking collectives  59.2 us (44%)
  Pallas kernels  44.6 us (33%)
  starting transfers between devices  14.5 us (11%)
  waiting for transfers between devices  8.92 us (7%)
  local copies, waits for them, and re-layouts  4.44 us (3%)
    all_to_all x2, blocking collectives, summed(): array = jnp.sum(lax.all_to_all(copies, axis, 0, 0), axis=0)  59.2 us
    pallas_call x1, Pallas kernels, pair_products(): pl.pallas_call(kernel, name='pairs', out_shape=[jax.ShapeDtypeStruct((rhs...  29.9 us
    ppermute x4, starting transfers between devices, passed_along(): return lax.ppermute(array, AXES, pairs)  14.5 us
    ppermute x4, waiting for transfers between devices, passed_along(): return lax.ppermute(array, AXES, pairs)  8.92 us
    pallas_call x1, Pallas kernels, finish(): pl.pallas_call(finish_kernel, name='finish', out_shape=[jax.ShapeDtypeStr...  7.62 us
    pallas_call x1, Pallas kernels, local_sums(): pl.pallas_call(sums_kernel, name='sums', out_shape=[jax.ShapeDtypeStruct(...  7.06 us
  transfers between devices with their start and end apart: 4, of which 2 were waited for; matrix products, arithmetic and copies ran while one was open for 1% of the time, Pallas kernels for 0%

profile of v1, /device:TPU:32, one launch (start us, length us, event | category | flops | bytes accessed | tf_op | source)
XLA Modules:
  0.0 133.1 jit_solution(12694986875736497384)
XLA Ops:
  0.6 0.9 slice.10
  1.6 6.1 %collective-permute-start.1 = (f32[16,3072]{1,0:T(8,128)S(1)}, f32[16,3072]{1,0:T(8,128)S(1)}, u32[]{:S(2)}, u32[]{:S(2)}) collective-permute-start(f32[16,3072]{1,0:T(8,128)S(1)} %slice.10), channel_id=1, source_target_pairs={{1,0},{2,1},{3,2},{4,3},{5,4},{6,5},{7,6},{8,7},{9,8},{10,9},{11,1... | collective-permute-start | bytes 589832 | tf_op jit(solution)/shard_map/ppermute | solution.py:416
  7.7 0.8 slice.11
  8.5 0.0 copy-start.3
  8.5 2.6 %collective-permute-start.2 = (f32[3,3072]{1,0:T(4,128)S(1)}, f32[3,3072]{1,0:T(4,128)S(1)}, u32[]{:S(2)}, u32[]{:S(2)}) collective-permute-start(f32[3,3072]{1,0:T(4,128)S(1)} %slice.11), channel_id=1, source_target_pairs={{1,0},{2,1},{3,2},{4,3},{5,4},{6,5},{7,6},{8,7},{9,8},{10,9},{11,1... | collective-permute-start | bytes 110600 | tf_op jit(solution)/shard_map/ppermute | solution.py:416
  11.1 0.0 copy-done.3
  11.1 2.1 %collective-permute-start = (s32[12]{0:T(128)S(1)}, s32[12]{0:T(128)S(1)}, u32[]{:S(2)}, u32[]{:S(2)}) collective-permute-start(s32[12]{0:T(128)S(1)} %bitcast.3), channel_id=1, source_target_pairs={{1,0},{2,1},{3,2},{4,3},{5,4},{6,5},{7,6},{8,7},{9,8},{10,9},{11,1... | collective-permute-start | bytes 152 | tf_op jit(solution)/shard_map/ppermute | solution.py:416
  13.2 1.3 collective-permute-done.refs_1_
  14.5 0.0 copy-start.4
  14.5 0.0 collective-permute-done.2.refs_5_
  14.5 0.0 copy-start.2
  14.5 0.0 collective-permute-done.1.refs_4_
  14.5 0.6 copy-done.4
  15.1 0.0 copy-done.2
  15.1 0.0 copy-start.1
  15.1 0.7 copy-done.1
  15.8 29.9 %pairs.1 = (f32[16,8192]{1,0:T(8,128)}, f32[16,3072]{1,0:T(8,128)}) custom-call(s32[32]{0:T(128)} %cnt.3, s32[12]{0:T(128)} %copy-done.4, f32[3,8192]{1,0:T(4,128)} %refs_2_.1, f32[16,8192]{1,0:T(8,128)} %dirs.3, f32[16,3072]{1,0:T(8,128)} %copy-done.1, f32[3,3072]{1,0:T(4,128)} %copy-done.2), custom_call_target="tpu_custom_call" | custom-call | tf_op jit(solution)/shard_map/pairs/pallas_call | solution.py:281
  45.7 3.8 %collective-permute-start.3 = (f32[16,3072]{1,0:T(8,128)}, f32[16,3072]{1,0:T(8,128)S(1)}, u32[]{:S(2)}, u32[]{:S(2)}) collective-permute-start(f32[16,3072]{1,0:T(8,128)} %get-tuple-element.8), channel_id=1, source_target_pairs={{0,1},{1,2},{2,3},{3,4},{4,5},{5,6},{6,7},{7,8},{8,9},{9,10},{10,1... | collective-permute-start | bytes 589832 | tf_op jit(solution)/shard_map/ppermute | solution.py:416
  49.5 7.6 %collective-permute-done.3.back = f32[16,3072]{1,0:T(8,128)S(1)} collective-permute-done((f32[16,3072]{1,0:T(8,128)}, f32[16,3072]{1,0:T(8,128)S(1)}, u32[]{:S(2)}, u32[]{:S(2)}) %collective-permute-start.3) | collective-permute-done | bytes 196640 | tf_op jit(solution)/shard_map/ppermute | solution.py:416
  57.2 0.0 copy-start
  57.2 0.7 copy-done
  57.8 7.1 %sums.1 = (f32[16,8192]{1,0:T(8,128)}, f32[16,128]{1,0:T(8,128)}) custom-call(s32[32]{0:T(128)} %cnt.3, f32[16,8192]{1,0:T(8,128)} %get-tuple-element.7.own, f32[16,3072]{1,0:T(8,128)} %copy-done, f32[1,8192]{1,0:T(1,128)} %bitcast.2, f32[16,8192]{1,0:T(8,128)} %dirs.3, f32[16,8192]{1,0:T(8,128)} %res.3, f32[32,8192]{1,0:T(8,128)} %ritz.1), custom_call_target="tpu_custom_call" | custom-call | tf_op jit(solution)/shard_map/sums/pallas_call | solution.py:354
  64.9 0.7 broadcast_in_dim.4
  65.6 31.7 %all_to_all.10 = f32[8,16,128]{2,1,0:T(8,128)S(1)} all-to-all(f32[8,16,128]{2,1,0:T(8,128)S(1)} %broadcast_in_dim.4), channel_id=1, replica_groups=mesh['region'=32,'cell'=8] {'cell'}, dimensions={0} | all-to-all | bytes 131072 | tf_op jit(solution)/shard_map/all_to_all | solution.py:422
  97.3 27.5 %all_to_all.11 = f32[32,16,128]{2,1,0:T(8,128)S(1)} all-to-all(f32[32,16,128]{2,1,0:T(8,128)S(1)} %broadcast_in_dim.5), channel_id=1, replica_groups=mesh['region'=32,'cell'=8] {'region'}, dimensions={0} | all-to-all | bytes 524288 | tf_op jit(solution)/shard_map/all_to_all | solution.py:422
  124.8 0.6 reduce_sum.19.sums
  125.5 7.6 %finish.1 = (f32[16,8192]{1,0:T(8,128)}, f32[16,8192]{1,0:T(8,128)}, f32[16,8192]{1,0:T(8,128)}) custom-call(s32[32]{0:T(128)} %cnt.3, f32[16,128]{1,0:T(8,128)} %reduce_sum.19.sums, f32[32,32]{1,0:T(8,128)} %gram.1, f32[16,8192]{1,0:T(8,128)} %get-tuple-element.10.image, f32[16,8192]{1,0:T(8,128)} %dirs.3, f32[16,8192]{1,0:T(8,128)} %res.3, ...), custom_call_target="tpu_custom_call" | custom-call | tf_op jit(solution)/shard_map/finish/pallas_call | solution.py:403
  (2 shorter events, 0.0 us)
Async XLA Ops:
  1.6 12.9 %collective-permute-start.1 = (f32[16,3072]{1,0:T(8,128)S(1)}, f32[16,3072]{1,0:T(8,128)S(1)}, u32[]{:S(2)}, u32[]{:S(2)}) collective-permute-start(f32[16,3072]{1,0:T(8,128)S(1)} %slice.10), channel_id=1, source_target_pairs={{1,0},{2,1},{3,2},{4,3},{5,4},{6,5},{7,6},{8,7},{9,8},{10,9},{11,1... | collective-permute-start | bytes 589832 | tf_op jit(solution)/shard_map/ppermute | solution.py:416
  8.5 2.6 %copy-start.3 = (s32[32]{0:T(128)S(1)}, s32[32]{0:T(128)}, u32[]{:S(2)}) copy-start(s32[32]{0:T(128)} %cnt.3) | copy-start | bytes 388
  8.5 6.0 %collective-permute-start.2 = (f32[3,3072]{1,0:T(4,128)S(1)}, f32[3,3072]{1,0:T(4,128)S(1)}, u32[]{:S(2)}, u32[]{:S(2)}) collective-permute-start(f32[3,3072]{1,0:T(4,128)S(1)} %slice.11), channel_id=1, source_target_pairs={{1,0},{2,1},{3,2},{4,3},{5,4},{6,5},{7,6},{8,7},{9,8},{10,9},{11,1... | collective-permute-start | bytes 110600 | tf_op jit(solution)/shard_map/ppermute | solution.py:416
  11.1 3.4 %collective-permute-start = (s32[12]{0:T(128)S(1)}, s32[12]{0:T(128)S(1)}, u32[]{:S(2)}, u32[]{:S(2)}) collective-permute-start(s32[12]{0:T(128)S(1)} %bitcast.3), channel_id=1, source_target_pairs={{1,0},{2,1},{3,2},{4,3},{5,4},{6,5},{7,6},{8,7},{9,8},{10,9},{11,1... | collective-permute-start | bytes 152 | tf_op jit(solution)/shard_map/ppermute | solution.py:416
  14.5 0.6 copy-start.4
  14.5 0.6 copy-start.2
  15.1 0.7 copy-start.1
  45.7 11.4 %collective-permute-start.3 = (f32[16,3072]{1,0:T(8,128)}, f32[16,3072]{1,0:T(8,128)S(1)}, u32[]{:S(2)}, u32[]{:S(2)}) collective-permute-start(f32[16,3072]{1,0:T(8,128)} %get-tuple-element.8), channel_id=1, source_target_pairs={{0,1},{1,2},{2,3},{3,4},{4,5},{5,6},{6,7},{7,8},{8,9},{9,10},{10,1... | collective-permute-start | bytes 589832 | tf_op jit(solution)/shard_map/ppermute | solution.py:416
  57.2 0.7 copy-start

commit v2 on v1

v2 whole, which is shorter than its diff:
```python
import jax
import jax.numpy as jnp
from jax import lax
from jax.experimental import pallas as pl
from jax.experimental.pallas import tpu as pltpu
from jax.sharding import PartitionSpec as P

PTS = 256
REACH = 12
KF = 48
FAR = 1e18
ROOM = 16.0
AXES = ("region", "cell")
F32 = jnp.float32
BF16 = jnp.bfloat16


def mm(x, y):
    return lax.dot_general(x, y, (((1,), (0,)), ((), ())), preferred_element_type=F32)


def mm_t(x, y):
    return lax.dot_general(x, y, (((1,), (1,)), ((), ())), preferred_element_type=F32)


def high(x):
    return x.astype(BF16).astype(F32)


def split3(x):
    h = high(x)
    m = high(x - h)
    return h, m, high(x - h - m)


def tile_of(scaled_square):
    s = jnp.maximum(scaled_square, 1e-30)
    t = s * lax.rsqrt(s)
    u = jnp.maximum(4.0 - t, 0.0)
    u2 = u * u
    return ((u2 * u2) * (t + 1.0)).astype(BF16)


def cols(block, size=PTS):
    return pl.ds(pl.multiple_of(block * size, size), size)


def with_norm(vec):
    row = lax.broadcasted_iota(jnp.int32, vec.shape, 0)
    return row, jnp.sum(vec * vec, axis=0, keepdims=True)


def weights_side(p):
    row, norm = with_norm(p)
    a = jnp.where(row == 3, norm, -2.0 * p)
    h, m, l = split3(a)
    one_h = jnp.where(row == 3, 1.0, h)
    one_m = jnp.where(row == 3, 1.0, m)
    return jnp.concatenate([h, m, one_h, one_m, l, one_h], axis=0).astype(BF16)


def rows_side(q):
    row, norm = with_norm(q)
    a = jnp.where(row == 3, norm, q)
    h, m, l = split3(a)
    one = jnp.where(row == 3, 1.0, h)
    mid_h = jnp.where(row == 3, h, m)
    return jnp.concatenate([one, one, mid_h, m, one, l], axis=0), norm


def pack(cells, cnt, off, dirs, pts, dc, pc):
    lane1 = lax.broadcasted_iota(jnp.int32, (1, PTS), 1)
    lane128 = lax.broadcasted_iota(jnp.int32, (1, 128), 1)
    dc[...] = jnp.zeros_like(dc)
    pc[...] = jnp.zeros_like(pc)

    def place(c, at):
        off[c] = at
        shift = at % 128
        base = pl.multiple_of((at // 128) * 128, 128)
        live = lane1 < cnt[c]
        dv = jnp.where(live, dirs[:, cols(c)], 0.0)
        pv = jnp.where(live, pts[:, cols(c)], 0.0)
        for ref, val in ((dc, dv), (pc, pv)):
            rows = val.shape[0]
            wide = jnp.concatenate([val, jnp.zeros((rows, 128), F32)], axis=1)
            wide = pltpu.roll(wide, shift, 1)
            old = ref[:rows, pl.ds(base, 128)]
            ref[:rows, pl.ds(base, 128)] = jnp.where(lane128 < shift, old, wide[:, :128])
            ref[:rows, pl.ds(base + 128, 256)] = wide[:, 128:]
        return at + cnt[c]

    return lax.fori_loop(0, cells, place, jnp.int32(0), unroll=4)


def prepare(blocks, pc, end, cen, fs):
    lane1 = lax.broadcasted_iota(jnp.int32, (1, PTS), 1)
    lane128 = lax.broadcasted_iota(jnp.int32, (1, 128), 1)

    def one(j, carry):
        low, top, far = carry
        here = pc[:, cols(j)]
        valid = j * PTS + lane1 < end
        lo = jnp.min(jnp.where(valid, here, FAR), axis=1, keepdims=True)
        hi = jnp.max(jnp.where(valid, here, -FAR), axis=1, keepdims=True)
        centre = jnp.where(lo <= hi, 0.5 * (lo + hi), 0.0)
        cen[pl.ds(pl.multiple_of(j * 8, 8), 8), :] = jnp.broadcast_to(centre, (8, 128))
        feats, norm = rows_side(4.0 * (here - centre))
        fs[cols(j), :] = feats.T.astype(BF16)
        low = jnp.where(lane128 == j, lo, low)
        top = jnp.where(lane128 == j, hi, top)
        return low, top, jnp.maximum(far, jnp.where(valid, norm, 0.0))

    start = (
        jnp.full((8, 128), FAR, F32),
        jnp.full((8, 128), -FAR, F32),
        jnp.zeros((1, PTS), F32),
    )
    low, top, far = lax.fori_loop(0, blocks, one, start, unroll=4)
    cen[pl.ds(blocks * 8, 8), :] = jnp.zeros((8, 128), F32)
    fs[pl.ds(blocks * PTS, PTS), :] = jnp.zeros((PTS, KF), BF16)
    wide = jnp.max(far, axis=1, keepdims=True) > 16.0 * ROOM
    return low, top, jnp.where(wide, 1, 0)


def square(v):
    return jnp.concatenate([v, jnp.zeros((120, 128), F32)], axis=0).T


def near(low_i, top_i, low_j, top_j):
    low_t, top_t = square(low_i), square(top_i)
    gap2 = jnp.zeros((128, 128), F32)
    for k in range(3):
        gap = jnp.maximum(
            low_j[k : k + 1] - top_t[:, k : k + 1], low_t[:, k : k + 1] - top_j[k : k + 1]
        )
        gap = jnp.maximum(gap, 0.0)
        gap2 = gap2 + gap * gap
    return gap2 <= 1.001


def as_rows(last):
    last = jnp.max(last.astype(F32), axis=1, keepdims=True)
    return jnp.broadcast_to(last, (128, 128)).T[:8].astype(jnp.int32)


def to_scalars(values, tab_v, tab_s, sem):
    tab_v[...] = values
    copy = pltpu.make_async_copy(tab_v, tab_s, sem)
    copy.start()
    copy.wait()


def sweep(first, end, begin, stop, spare, spread, side_i, side_j, acc_i, acc_j, bufs):
    pc_i, db_i = side_i
    pc_j, db_j, fs_j, cen_j = side_j
    f0, f1, s0, s1, w0, w1 = bufs
    zero = jnp.int32(0)

    def enter(i):
        i = jnp.where(i >= end, spare[0], i)
        return i, jnp.where(i == spare[0], spare[1], begin(i))

    def following(i, j):
        n = j + 1
        over = (n >= stop(i)) | (i == spare[0])
        i2, j2 = enter(i + 1)
        return jnp.where(over, i2, i), jnp.where(over, j2, n)

    def stage0(i, j, f):
        c = cen_j[pl.ds(pl.multiple_of(j * 8, 8), 8), :]
        f[...] = weights_side(4.0 * (pc_i[:, cols(i)] - jnp.concatenate([c, c], axis=1)))

    def stage1(j, f, s):
        s[...] = mm(fs_j[cols(j), :], f[...])

    def stage2(s, w):
        w[...] = tile_of(s[...])

    same = acc_j is not None and db_i is db_j

    def stage3(i, j, w):
        tile = w[...]
        acc_i[:, cols(i)] += mm(db_j[:, cols(j)], tile)
        other = mm_t(db_i[:, cols(i)], tile)
        if same:
            other = other * jnp.where(j > i, 1.0, 0.0)
        acc_j[:, cols(j)] += other

    total = lax.fori_loop(first, end, lambda i, n: n + stop(i) - begin(i), zero)
    ia, ja = enter(jnp.int32(first))

    @pl.when(spread == 0)
    def _():
        w1[...] = jnp.zeros_like(w1)
        ib, jb = following(ia, ja)
        stage0(ia, ja, f0)
        stage1(ja, f0, s0)
        stage0(ib, jb, f1)

        def two(_, carry):
            iz, jz, i0, j0, i1, j1 = carry
            i2, j2 = following(i1, j1)
            stage0(i2, j2, f0)
            stage1(j1, f1, s1)
            stage2(s0, w0)
            stage3(iz, jz, w1)
            i3, j3 = following(i2, j2)
            stage0(i3, j3, f1)
            stage1(j2, f0, s0)
            stage2(s1, w1)
            stage3(i0, j0, w0)
            return i1, j1, i2, j2, i3, j3

        last = (jnp.int32(spare[0]), jnp.int32(spare[1]))
        lax.fori_loop(0, total // 2 + 1, two, last + (ia, ja, ib, jb))

    @pl.when(spread != 0)
    def _():
        def one(_, carry):
            i, j = carry
            pj = pc_j[:, cols(j)].T
            pi = pc_i[:, cols(i)]
            for h in range(0, PTS, 64):
                s = jnp.zeros((64, PTS), F32)
                for k in range(3):
                    d = 4.0 * (pj[h : h + 64, k : k + 1] - pi[k : k + 1, :])
                    s = s + d * d
                w0[pl.ds(h, 64), :] = tile_of(s)
            stage3(i, j, w0)
            return following(i, j)

        lax.fori_loop(0, total, one, (ia, ja))


def strips_of(cells, cnt):
    return (lax.fori_loop(0, cells, lambda c, n: n + cnt[c], jnp.int32(0)) + (PTS - 1)) // PTS


def early(strips):
    return (strips * EARLY) // 16


def head_kernel(cells, cnt, pts, dirs, db, pc, fs, cen, box, tab, acc_i, acc_j, off, dc, *rest):
    *bufs, tab_s, sem = rest
    acc_i[...] = jnp.zeros_like(acc_i)
    acc_j[...] = jnp.zeros_like(acc_j)
    own_end = pack(cells, cnt, off, dirs, pts, dc, pc)
    strips = (own_end + (PTS - 1)) // PTS
    db[...] = dc[...].astype(BF16)
    low, top, spread = prepare(cells, pc, own_end, cen, fs)
    box[0:8, :] = low
    box[8:16, :] = top
    ri = lax.broadcasted_iota(jnp.int32, (128, 128), 0)
    rj = lax.broadcasted_iota(jnp.int32, (128, 128), 1)
    need = near(low, top, low, top) & (rj > ri)
    stop = as_rows(jnp.where(need, rj + 1, ri + 1))
    lane128 = lax.broadcasted_iota(jnp.int32, (1, 128), 1)
    to_scalars(jnp.where(lane128 == 127, spread, stop), tab, tab_s, sem)
    side = (pc, db, fs, cen)
    sweep(
        0, early(strips), lambda i: i, lambda i: tab_s[0, i], (cells, cells), tab_s[0, 127],
        side[:2], side, acc_i, acc_j, bufs,
    )


def edge_kernel(cells, halo_cells, cnt, db, pc, box, tab, piece, halo, acc_i, hdb, hfs, hcen, tab_v, *rest):
    *bufs, tab_s, sem = rest
    strips = strips_of(cells, cnt)
    acc_i[...] = jnp.zeros_like(acc_i)
    halo[...] = jnp.zeros_like(halo)
    rhs = hdb.shape[0]
    hdb[:, : halo_cells * PTS] = piece[:rhs, :].astype(BF16)
    hdb[:, halo_cells * PTS :] = jnp.zeros((rhs, PTS), BF16)
    hpc = piece.at[rhs : rhs + 8]
    low, top, spread = prepare(halo_cells, hpc, halo_cells * PTS, hcen, hfs)
    ri = lax.broadcasted_iota(jnp.int32, (128, 128), 0)
    rj = lax.broadcasted_iota(jnp.int32, (128, 128), 1)
    need = near(box[0:8, :], box[8:16, :], low, top) & (rj < halo_cells) & (ri < cells)
    stop = as_rows(jnp.where(need, rj + 1, 0))
    lane128 = lax.broadcasted_iota(jnp.int32, (1, 128), 1)
    first = jnp.min(jnp.where(need, ri, 127).astype(F32), axis=(0, 1), keepdims=True)
    stop = jnp.where(lane128 == 126, first.astype(jnp.int32), stop)
    wide = jnp.where((tab[...] != 0) & (lane128 == 127), 1, 0)
    to_scalars(jnp.where(lane128 == 127, spread + wide, stop), tab_v, tab_s, sem)
    sweep(
        jnp.minimum(tab_s[0, 126], strips), strips, lambda i: jnp.int32(0),
        lambda i: jnp.maximum(tab_s[0, i], 1), (cells, halo_cells), tab_s[0, 127],
        (pc, db), (hpc, hdb, hfs, hcen), acc_i, halo, bufs,
    )
    halo[:, : halo_cells * PTS] = halo[:, : halo_cells * PTS] * (1.0 / 256.0)


def tail_kernel(cells, cnt, db, pc, fs, cen, tab, a1, a2, b1, own, off, acc_i, acc_j, *rest):
    bufs = rest
    lane1 = lax.broadcasted_iota(jnp.int32, (1, PTS), 1)
    acc_i[...] = a1[...] + a2[...]
    acc_j[...] = b1[...]

    def place(c, at):
        off[c] = at
        return at + cnt[c]

    end = lax.fori_loop(0, cells, place, jnp.int32(0))
    strips = (end + (PTS - 1)) // PTS
    side = (pc, db, fs, cen)
    sweep(
        early(strips), strips, lambda i: i, lambda i: tab[0, i], (cells, cells), tab[0, 127],
        side[:2], side, acc_i, acc_j, bufs,
    )

    def take(c, _):
        at = off[c]
        base = pl.multiple_of((at // 128) * 128, 128)
        both = acc_i[:, pl.ds(base, 384)] + acc_j[:, pl.ds(base, 384)]
        back = pltpu.roll(both, 384 - at % 128, 1)[:, :PTS] * (1.0 / 256.0)
        own[:, cols(c)] = jnp.where(lane1 < cnt[c], back, 0.0)
        return 0

    lax.fori_loop(0, cells, take, 0, unroll=4)


def piece_kernel(cells, cnt, pts, dirs, piece):
    rhs = dirs.shape[0]
    lane1 = lax.broadcasted_iota(jnp.int32, (1, PTS), 1)
    piece[rhs:, :] = jnp.zeros_like(piece[rhs:, :])
    for c in range(cells):
        at = slice(c * PTS, (c + 1) * PTS)
        live = lane1 < cnt[c]
        piece[:rhs, at] = jnp.where(live, dirs[:, at], 0.0)
        piece[rhs : rhs + 3, at] = jnp.where(live, pts[:, at], pts[:, c * PTS : c * PTS + 1])


VM = pl.BlockSpec(memory_space=pltpu.VMEM)
SM = pl.BlockSpec(memory_space=pltpu.SMEM)
EARLY = 4


def params(mib):
    return pltpu.CompilerParams(vmem_limit_bytes=mib << 20)


def buffers():
    return [
        pltpu.VMEM((KF, PTS), BF16),
        pltpu.VMEM((KF, PTS), BF16),
        pltpu.VMEM((PTS, PTS), F32),
        pltpu.VMEM((PTS, PTS), F32),
        pltpu.VMEM((PTS, PTS), BF16),
        pltpu.VMEM((PTS, PTS), BF16),
    ]


def cost(units):
    return pl.CostEstimate(flops=units * 60_000_000, bytes_accessed=4_000_000, transcendentals=units * 65536)


def pair_products(counts, points, direction):
    cells = counts.shape[0]
    rhs = direction.shape[0]
    width = min(cells, REACH)
    blocks = cells + 1
    wide = blocks * PTS + 256
    shape = jax.ShapeDtypeStruct

    piece = pl.pallas_call(
        lambda *refs: piece_kernel(width, *refs),
        name="piece",
        grid=(1,),
        out_shape=shape((rhs + 8, width * PTS), F32),
        in_specs=[
            SM,
            pl.BlockSpec((3, width * PTS), lambda i: (0, 0)),
            pl.BlockSpec((rhs, width * PTS), lambda i: (0, 0)),
        ],
        out_specs=pl.BlockSpec((rhs + 8, width * PTS), lambda i: (0, 0)),
        compiler_params=params(8),
    )(counts, points, direction)
    piece = passed_along(piece, -1)
    db, pc, fs, cen, box, tab, acc_i, acc_j = pl.pallas_call(
        lambda *refs: head_kernel(cells, *refs),
        name="head",
        out_shape=[
            shape((rhs, wide), BF16),
            shape((8, wide), F32),
            shape((blocks * PTS, KF), BF16),
            shape((blocks * 8, 128), F32),
            shape((16, 128), F32),
            shape((8, 128), jnp.int32),
            shape((rhs, wide), F32),
            shape((rhs, wide), F32),
        ],
        in_specs=[SM, VM, VM],
        out_specs=[VM] * 8,
        scratch_shapes=[pltpu.SMEM((cells,), jnp.int32), pltpu.VMEM((rhs, wide), F32)]
        + buffers()
        + [pltpu.SMEM((8, 128), jnp.int32), pltpu.SemaphoreType.DMA],
        compiler_params=params(12),
        cost_estimate=cost(100),
    )(counts, points, direction)
    halo, acc_e = pl.pallas_call(
        lambda *refs: edge_kernel(cells, width, *refs),
        name="edge",
        out_shape=[shape((rhs, (width + 1) * PTS), F32), shape((rhs, wide), F32)],
        in_specs=[SM] + [VM] * 5,
        out_specs=[VM] * 2,
        scratch_shapes=[
            pltpu.VMEM((rhs, (width + 1) * PTS), BF16),
            pltpu.VMEM(((width + 1) * PTS, KF), BF16),
            pltpu.VMEM(((width + 1) * 8, 128), F32),
            pltpu.VMEM((8, 128), jnp.int32),
        ]
        + buffers()
        + [pltpu.SMEM((8, 128), jnp.int32), pltpu.SemaphoreType.DMA],
        compiler_params=params(12),
        cost_estimate=cost(70),
    )(counts, db, pc, box, tab, piece)
    back = passed_along(halo, 1)
    own = pl.pallas_call(
        lambda *refs: tail_kernel(cells, *refs),
        name="tail",
        out_shape=shape((rhs, cells * PTS), F32),
        in_specs=[SM] + [VM] * 4 + [SM] + [VM] * 3,
        out_specs=VM,
        scratch_shapes=[
            pltpu.SMEM((cells,), jnp.int32),
            pltpu.VMEM((rhs, wide), F32),
            pltpu.VMEM((rhs, wide), F32),
        ]
        + buffers(),
        compiler_params=params(12),
        cost_estimate=cost(180),
    )(counts, db, pc, fs, cen, tab, acc_i, acc_e, acc_j)
    return own, back


def sums_kernel(cnt, own, back, nug, dirs, res, ritz, image, sums):
    cells = own.shape[1] // PTS
    halo_cells = back.shape[1] // PTS - 1
    lane1 = lax.broadcasted_iota(jnp.int32, (1, PTS), 1)

    def of_cell(c, part, extra):
        live = lane1 < cnt[c]
        d = jnp.where(live, dirs[:, cols(c)], 0.0)
        r = jnp.where(live, res[:, cols(c)], 0.0)
        k = own[:, cols(c)]
        if extra:
            k = k + back[:, cols(c)]
        im = jnp.where(live, nug[:, cols(c)] * d + k, 0.0)
        image[:, cols(c)] = im
        dk, rr, ri, ii, prod = part
        both = jnp.concatenate([r, im], axis=0)
        bh = high(both)
        z = ritz[:, cols(c)]
        zh = high(z)
        left = jnp.concatenate([bh, both - bh], axis=0).astype(BF16)
        right = jnp.concatenate([zh, z - zh], axis=0).astype(BF16)
        return dk + d * im, rr + r * r, ri + r * im, ii + im * im, prod + mm_t(left, right)

    rhs = own.shape[0]
    zero = jnp.zeros((rhs, PTS), F32)
    part = (zero, zero, zero, zero, jnp.zeros((4 * rhs, 2 * ritz.shape[0]), F32))
    part = lax.fori_loop(0, halo_cells, lambda c, p: of_cell(c, p, True), part, unroll=4)
    part = lax.fori_loop(halo_cells, cells, lambda c, p: of_cell(c, p, False), part, unroll=4)
    dots = [jnp.sum(p, axis=1, keepdims=True) for p in part[:4]]
    prod = part[4]
    n = ritz.shape[0]
    h = 2 * rhs
    prod = prod[:h, :n] + prod[:h, n:] + prod[h:, :n]
    sums[...] = jnp.zeros_like(sums)
    sums[:, :n] = prod[:rhs]
    sums[:, n : 2 * n] = prod[rhs:]
    for k in range(4):
        sums[:, 2 * n + k : 2 * n + k + 1] = dots[k]


def local_sums(counts, own, back, nugget, direction, residual, ritz_image):
    return pl.pallas_call(
        sums_kernel,
        name="sums",
        out_shape=[
            jax.ShapeDtypeStruct(own.shape, F32),
            jax.ShapeDtypeStruct((own.shape[0], 128), F32),
        ],
        in_specs=[SM] + [VM] * 6,
        out_specs=[VM, VM],
        compiler_params=params(12),
    )(counts, own, back, nugget, direction, residual, ritz_image)


def finish_kernel(cnt, sums, gram, image, dirs, res, sol, basis, sol_out, res_out, dir_out):
    cells = image.shape[1] // PTS
    n = gram.shape[0]
    lane1 = lax.broadcasted_iota(jnp.int32, (1, PTS), 1)
    curvature, rr, ri, ii = (sums[:, 2 * n + k : 2 * n + k + 1] for k in range(4))
    step = rr / curvature
    growth = (rr + step * (step * ii - 2.0 * ri)) / rr
    projected = sums[:, :n] - step * sums[:, n : 2 * n]
    coef = lax.dot_general(
        projected,
        gram[...],
        (((1,), (1,)), ((), ())),
        precision=lax.Precision.HIGHEST,
        preferred_element_type=F32,
    )
    ch = high(coef)
    left = jnp.concatenate([ch, ch, coef - ch], axis=1).astype(BF16)

    def of_cell(c, _):
        live = lane1 < cnt[c]
        d = jnp.where(live, dirs[:, cols(c)], 0.0)
        r = jnp.where(live, res[:, cols(c)], 0.0)
        s = jnp.where(live, sol[:, cols(c)], 0.0)
        b = basis[:, cols(c)]
        bh = high(b)
        right = jnp.concatenate([bh, b - bh, bh], axis=0).astype(BF16)
        new = r - step * image[:, cols(c)]
        sol_out[:, cols(c)] = s + step * d
        res_out[:, cols(c)] = new
        dir_out[:, cols(c)] = jnp.where(live, growth * d + new - mm(left, right), 0.0)
        return 0

    lax.fori_loop(0, cells, of_cell, 0, unroll=4)


def finish(counts, sums, gram, image, direction, residual, solution, basis):
    return pl.pallas_call(
        finish_kernel,
        name="finish",
        out_shape=[jax.ShapeDtypeStruct(image.shape, F32)] * 3,
        in_specs=[SM] + [VM] * 7,
        out_specs=[VM] * 3,
        compiler_params=params(12),
    )(counts, sums, gram, image, direction, residual, solution, basis)


def passed_along(array, by):
    length = lax.axis_size(AXES)
    pairs = [(i, i + by) for i in range(length) if 0 <= i + by < length]
    return lax.ppermute(array, AXES, pairs)


def summed(array):
    for axis in ("cell", "region"):
        copies = jnp.broadcast_to(array[None], (lax.axis_size(axis),) + array.shape)
        array = jnp.sum(lax.all_to_all(copies, axis, 0, 0), axis=0)
    return array


def local(
    points,
    cell_counts,
    pair_cells,
    pair_counts,
    nugget,
    solution,
    residual,
    direction,
    ritz_basis,
    ritz_image,
    inverse_gram,
):
    own, back = pair_products(cell_counts, points, direction)
    image, sums = local_sums(
        cell_counts, own, back, nugget.reshape(1, -1), direction, residual, ritz_image
    )
    return tuple(
        finish(
            cell_counts,
            summed(sums),
            inverse_gram,
            image,
            direction,
            residual,
            solution,
            ritz_basis,
        )
    )


def solution(mesh):
    split = P(None, AXES)
    line = P(AXES)
    in_specs = (split, line, split, line, line, split, split, split, split, split, P())
    return jax.shard_map(
        local, mesh=mesh, in_specs=in_specs, out_specs=(split,) * 3, check_vma=False
    )
```

time: 134 us -> 104 us (0.78)
  blocking collectives: 59.2 us -> 29.7 us
  Pallas kernels: 44.6 us -> 59.8 us
  waiting for transfers between devices: 8.92 us -> 0.01 us
  starting transfers between devices: 14.5 us -> 8.02 us
    all_to_all x2, blocking collectives: 59.2 us -> 29.7 us  [summed(): array = jnp.sum(lax.all_to_all(copies, axis, 0, 0), axis=0)]
    pallas_call x1 -> x4, Pallas kernels: 29.9 us -> 54.4 us  [the longest x1 26.6 us: pair_products(): pl.pallas_call(lambda *refs: tail_kernel(cells, *refs), name='tail', out_...]
    ppermute x4 -> x2, waiting for transfers between devices: 8.92 us -> 0.01 us  [passed_along(): return lax.ppermute(array, AXES, pairs)]
    ppermute x4 -> x2, starting transfers between devices: 14.5 us -> 8.02 us  [passed_along(): return lax.ppermute(array, AXES, pairs)]
    pallas_call x1, Pallas kernels: 7.06 us -> 2.24 us  [local_sums(): pl.pallas_call(sums_kernel, name='sums', out_shape=[jax.ShapeDtypeStruct(...]
    pallas_call x1, Pallas kernels: 7.62 us -> 3.23 us  [finish(): pl.pallas_call(finish_kernel, name='finish', out_shape=[jax.ShapeDtypeStr...]
    unnamed x10 -> x28, local copies, waits for them, and re-layouts: 1.97 us -> 5.24 us
    slice x2 -> x0, local copies, waits for them, and re-layouts: 1.75 us -> none  [the longest x1 0.94 us: local(): halo_dirs = passed_along(direction[:, :width * PTS], -1)]
  transfers between devices with their start and end apart: 4 -> 2, of which waited for: 2 -> 0; matrix products, arithmetic and copies ran while one was open for 1% -> 0% of each run, Pallas kernels for 0% -> 40%
where the time goes in v2:
time: 104 us
  Pallas kernels  59.8 us (58%)
  blocking collectives  29.7 us (29%)
  starting transfers between devices  8.02 us (8%)
  local copies, waits for them, and re-layouts  5.29 us (5%)
    all_to_all x2, blocking collectives, summed(): array = jnp.sum(lax.all_to_all(copies, axis, 0, 0), axis=0)  29.7 us
    pallas_call x1, Pallas kernels, pair_products(): pl.pallas_call(lambda *refs: tail_kernel(cells, *refs), name='tail', out_...  26.6 us
    pallas_call x1, Pallas kernels, pair_products(): pl.pallas_call(lambda *refs: head_kernel(cells, *refs), name='head', out_...  15.3 us
    pallas_call x1, Pallas kernels, pair_products(): pl.pallas_call(lambda *refs: edge_kernel(cells, width, *refs), name='edge...  11.8 us
    ppermute x2, starting transfers between devices, passed_along(): return lax.ppermute(array, AXES, pairs)  8.02 us
    unnamed x28, local copies, waits for them, and re-layouts  5.24 us
    pallas_call x1, Pallas kernels, finish(): pl.pallas_call(finish_kernel, name='finish', out_shape=[jax.ShapeDtypeStr...  3.23 us
    pallas_call x1, Pallas kernels, local_sums(): pl.pallas_call(sums_kernel, name='sums', out_shape=[jax.ShapeDtypeStruct(...  2.24 us
  transfers between devices with their start and end apart: 2, of which 0 were waited for; matrix products, arithmetic and copies ran while one was open for 0% of the time, Pallas kernels for 40%

profile of v2, /device:TPU:32, one launch (start us, length us, event | category | flops | bytes accessed | tf_op | source)
XLA Modules:
  0.0 103.8 jit_solution(2818186238549314287)
XLA Ops:
  0.6 0.0 copy-start
  0.6 1.0 copy-done
  1.7 0.0 copy-start.7
  1.7 0.9 copy-done.7
  2.6 0.0 copy-start.11
  2.6 0.7 copy-done.11
  3.2 0.6 piece.1
  3.9 6.1 %collective-permute-start = (f32[24,3072]{1,0:T(8,128)S(1)}, f32[24,3072]{1,0:T(8,128)S(1)}, u32[]{:S(2)}, u32[]{:S(2)}) collective-permute-start(f32[24,3072]{1,0:T(8,128)S(1)} %piece.1), channel_id=1, source_target_pairs={{1,0},{2,1},{3,2},{4,3},{5,4},{6,5},{7,6},{8,7},{9,8},{10,9},{11,1... | collective-permute-start | bytes 884744 | tf_op jit(solution)/shard_map/ppermute | solution.py:540
  10.0 0.0 copy-start.1
  10.0 1.0 copy-done.1
  11.0 0.0 copy-start.8
  11.0 0.9 copy-done.8
  11.9 0.0 copy-start.12
  11.9 0.7 copy-done.12
  12.6 15.3 %head.1 = (bf16[16,8704]{1,0:T(8,128)(2,1)S(1)}, f32[8,8704]{1,0:T(8,128)S(1)}, bf16[8448,48]{1,0:T(8,128)(2,1)S(1)}, f32[264,128]{1,0:T(8,128)S(1)}, f32[16,128...) custom-call(s32[32]{0:T(128)S(1)} %copy-done.12, ...), custom_call_target="tpu_custom_call" | custom-call | flops 6000000000 | bytes 4000000 | tf_op jit(solution)/shard_map/head/pallas_call | solution.py:380
  27.9 0.0 collective-permute-done.refs_5_
  27.9 11.8 %edge.1 = (f32[16,3328]{1,0:T(8,128)S(1)}, f32[16,8704]{1,0:T(8,128)S(1)}) custom-call(s32[32]{0:T(128)S(1)} %copy-done.12, bf16[16,8704]{1,0:T(8,128)(2,1)S(1)} %get-tuple-element.15.refs_1_, f32[8,8704]{1,0:T(8,128)S(1)} %get-tuple-element.16.refs_2_, f32[16,128]{1,0:T(8,128)S(1)} %get-tuple-element.21.refs_3_, ...), custom_call_target="tpu_custom_call" | custom-call | flops 4200000000 | bytes 4000000 | tf_op jit(solution)/shard_map/edge/pallas_call | solution.py:401
  39.7 1.9 %collective-permute-start.1 = (f32[16,3328]{1,0:T(8,128)S(1)}, f32[16,3328]{1,0:T(8,128)S(1)}, u32[]{:S(2)}, u32[]{:S(2)}) collective-permute-start(f32[16,3328]{1,0:T(8,128)S(1)} %get-tuple-element.24), channel_id=1, source_target_pairs={{0,1},{1,2},{2,3},{3,4},{4,5},{5,6},{6,7},{7,8},{8,9},{9,10},{10,1... | collective-permute-start | bytes 638984 | tf_op jit(solution)/shard_map/ppermute | solution.py:540
  41.6 0.0 copy-start.2
  41.6 0.0 copy-start.3
  41.7 0.0 copy-start.4
  41.7 0.0 copy-start.9
  41.7 26.6 %tail.1.own = f32[16,8192]{1,0:T(8,128)S(1)} custom-call(s32[32]{0:T(128)S(1)} %copy-done.12, bf16[16,8704]{1,0:T(8,128)(2,1)S(1)} %get-tuple-element.15.refs_1_, f32[8,8704]{1,0:T(8,128)S(1)} %get-tuple-element.16.refs_2_, bf16[8448,48]{1,0:T(8,128)(2,1)S(1)} %get-tuple-element.17.refs_3_, f32[264,128]{1,0:T(8,128)S(1)} %get-tuple-element.18.refs_4_, ...), custom_call_target="tpu_custom_call" | custom-call | flops 10800000000 | bytes 4000000 | tf_op jit(solution)/shard_map/tail/pallas_call | solution.py:419
  68.3 0.0 copy-start.5
  68.3 0.0 copy-start.6
  68.4 0.0 copy-start.10
  68.4 0.0 copy-start.13
  68.4 0.0 collective-permute-done.1.back
  68.4 0.0 copy-done.2
  68.4 0.0 copy-done.3
  68.4 0.0 copy-done.4
  68.4 0.0 copy-done.9
  68.4 2.2 %sums.1 = (f32[16,8192]{1,0:T(8,128)S(1)}, f32[16,128]{1,0:T(8,128)S(1)}) custom-call(s32[32]{0:T(128)S(1)} %copy-done.12, f32[16,8192]{1,0:T(8,128)S(1)} %tail.1.own, f32[16,3328]{1,0:T(8,128)S(1)} %collective-permute-done.1.back, f32[1,8192]{1,0:T(1,128)S(1)} %bitcast.1, f32[16,8192]{1,0:T(8,128)S(1)} %copy-done.2, f32[16,8192]{1,0:T(8,128)S(1)} %copy-done.3, ...), custom_call_target="tpu_custom_call" | custom-call | tf_op jit(solution)/shard_map/sums/pallas_call | solution.py:478
  70.7 8.0 %all_to_all.10 = f32[8,16,128]{2,1,0:T(8,128)S(1)} all-to-all(f32[8,16,128]{2,1,0:T(8,128)S(1)} %broadcast_in_dim.4), channel_id=1, replica_groups=mesh['region'=32,'cell'=8] {'cell'}, dimensions={0} | all-to-all | bytes 131072 | tf_op jit(solution)/shard_map/all_to_all | solution.py:546
  78.7 21.7 %all_to_all.11 = f32[32,16,128]{2,1,0:T(8,128)S(1)} all-to-all(f32[32,16,128]{2,1,0:T(8,128)S(1)} %broadcast_in_dim.5), channel_id=1, replica_groups=mesh['region'=32,'cell'=8] {'region'}, dimensions={0} | all-to-all | bytes 524288 | tf_op jit(solution)/shard_map/all_to_all | solution.py:546
  100.5 0.0 copy-done.5
  100.5 0.0 copy-done.6
  100.5 0.0 copy-done.10
  100.5 0.0 copy-done.13
  100.5 3.2 %finish.1 = (f32[16,8192]{1,0:T(8,128)}, f32[16,8192]{1,0:T(8,128)}, f32[16,8192]{1,0:T(8,128)}) custom-call(s32[32]{0:T(128)S(1)} %copy-done.13, f32[16,128]{1,0:T(8,128)S(1)} %reduce_sum.19.sums, f32[32,32]{1,0:T(8,128)S(1)} %copy-done.10, f32[16,8192]{1,0:T(8,128)S(1)} %get-tuple-element.26.image, f32[16,8192]{1,0:T(8,128)S(1)} %copy-done.2, ...), custom_call_target="tpu_custom_call" | custom-call | tf_op jit(solution)/shard_map/finish/pallas_call | solution.py:527
  (4 shorter events, 0.1 us)
Async XLA Ops:
  0.6 1.0 %copy-start = (f32[16,8192]{1,0:T(8,128)S(1)}, f32[16,8192]{1,0:T(8,128)}, u32[]{:S(2)}) copy-start(f32[16,8192]{1,0:T(8,128)} %dirs.3) | copy-start | bytes 1572868
  1.7 0.9 copy-start.7
  2.6 0.7 copy-start.11
  3.9 24.0 %collective-permute-start = (f32[24,3072]{1,0:T(8,128)S(1)}, f32[24,3072]{1,0:T(8,128)S(1)}, u32[]{:S(2)}, u32[]{:S(2)}) collective-permute-start(f32[24,3072]{1,0:T(8,128)S(1)} %piece.1), channel_id=1, source_target_pairs={{1,0},{2,1},{3,2},{4,3},{5,4},{6,5},{7,6},{8,7},{9,8},{10,9},{11,1... | collective-permute-start | bytes 884744 | tf_op jit(solution)/shard_map/ppermute | solution.py:540
  10.0 1.0 %copy-start.1 = (f32[16,8192]{1,0:T(8,128)S(1)}, f32[16,8192]{1,0:T(8,128)}, u32[]{:S(2)}) copy-start(f32[16,8192]{1,0:T(8,128)} %dirs.3) | copy-start | bytes 1572868
  11.0 0.9 copy-start.8
  11.9 0.7 copy-start.12
  39.7 28.7 %collective-permute-start.1 = (f32[16,3328]{1,0:T(8,128)S(1)}, f32[16,3328]{1,0:T(8,128)S(1)}, u32[]{:S(2)}, u32[]{:S(2)}) collective-permute-start(f32[16,3328]{1,0:T(8,128)S(1)} %get-tuple-element.24), channel_id=1, source_target_pairs={{0,1},{1,2},{2,3},{3,4},{4,5},{5,6},{6,7},{7,8},{8,9},{9,10},{10,1... | collective-permute-start | bytes 638984 | tf_op jit(solution)/shard_map/ppermute | solution.py:540
  41.6 26.8 %copy-start.2 = (f32[16,8192]{1,0:T(8,128)S(1)}, f32[16,8192]{1,0:T(8,128)}, u32[]{:S(2)}) copy-start(f32[16,8192]{1,0:T(8,128)} %dirs.3) | copy-start | bytes 1572868
  41.6 26.8 %copy-start.3 = (f32[16,8192]{1,0:T(8,128)S(1)}, f32[16,8192]{1,0:T(8,128)}, u32[]{:S(2)}) copy-start(f32[16,8192]{1,0:T(8,128)} %res.3) | copy-start | bytes 1572868
  41.7 26.8 %copy-start.4 = (f32[32,8192]{1,0:T(8,128)S(1)}, f32[32,8192]{1,0:T(8,128)}, u32[]{:S(2)}) copy-start(f32[32,8192]{1,0:T(8,128)} %ritz.1) | copy-start | bytes 3145732
  41.7 26.8 %copy-start.9 = (f32[8192]{0:T(1024)S(1)}, f32[8192]{0:T(1024)}, u32[]{:S(2)}) copy-start(f32[8192]{0:T(1024)} %param.13) | copy-start | bytes 98308
  68.3 32.2 %copy-start.5 = (f32[32,8192]{1,0:T(8,128)S(1)}, f32[32,8192]{1,0:T(8,128)}, u32[]{:S(2)}) copy-start(f32[32,8192]{1,0:T(8,128)} %basis.1) | copy-start | bytes 3145732
  68.3 32.2 %copy-start.6 = (f32[16,8192]{1,0:T(8,128)S(1)}, f32[16,8192]{1,0:T(8,128)}, u32[]{:S(2)}) copy-start(f32[16,8192]{1,0:T(8,128)} %sol.1) | copy-start | bytes 1572868
  68.4 32.2 %copy-start.10 = (f32[32,32]{1,0:T(8,128)S(1)}, f32[32,32]{1,0:T(8,128)}, u32[]{:S(2)}) copy-start(f32[32,32]{1,0:T(8,128)} %gram.1) | copy-start | bytes 12292
  68.4 32.2 %copy-start.13 = (s32[32]{0:T(128)S(1)}, s32[32]{0:T(128)}, u32[]{:S(2)}) copy-start(s32[32]{0:T(128)} %cnt.3) | copy-start | bytes 388
